TPU v7x, 32 devices: a whole 2x2x4 slice. The times are simulated.
32 devices in a mesh: dp: 4 (over x, core), cls: 8 (over z, y).
Axes of the slice: x: 2, y: 2, z: 4, core: 2. Of those that a mesh axis runs over, the one named last changes fastest.
Arguments:
- faces: bfloat16 [2, 32, 512], P(None, ('dp', 'cls')), may hold values from -2 to 2
- labels: int32 [2, 32], replicated, may hold values from 0 to 16383, as said below
- centres: bfloat16 [16384, 512], P(('dp', 'cls')), may hold values from -4 to 4
- momentum: bfloat16 [16384, 512], P(('dp', 'cls')), may hold values from -3 to 3
Outputs:
- face_grad: float32 [2, 32, 512], P(None, ('dp', 'cls'))
- new_centres: bfloat16 [16384, 512], P(('dp', 'cls'))
- new_momentum: bfloat16 [16384, 512], P(('dp', 'cls'))
Inputs may be any that keep to these rules, and one draw needn't show every extreme that they name: `labels`: some face has class 0 and some face has class 16384 - 1.
All inputs are finite; a program needn't handle non-finite values.
Results may differ from a plain program's by a relative error of at most 0.0057.
Values may be sent and summed in bfloat16 or wider, within the bound.
A program may use at most 64 MiB of HBM per device.

v0:
```python
import jax
import jax.numpy as jnp
from jax import lax
from jax.sharding import PartitionSpec as P

SCALE = 30.0
MARGIN = 0.4
POS_WEIGHT = 0.7
BIAS = 6.5
EPS = 1e-06
MOMENTUM_RATE = 0.9
LEARN_RATE = 0.1
DECAY = 0.0005


def as_sent(x):

    def short(part):
        return part.astype(jnp.bfloat16) if part.dtype == jnp.float32 else part

    return jax.tree.map(short, x)


def logit_grad(cosine, positive):
    halfway = (cosine + 1.0) * 0.5
    shaped = 2.0 * halfway * halfway * halfway - 1.0
    slopes = 3.0 * halfway * halfway
    pos_term = -POS_WEIGHT * SCALE * jax.nn.sigmoid(-(SCALE * (shaped - MARGIN) + BIAS))
    neg_term = (1.0 - POS_WEIGHT) * SCALE * jax.nn.sigmoid(SCALE * (shaped + MARGIN) + BIAS)
    return (jnp.where(positive, pos_term, neg_term) * slopes).astype(jnp.bfloat16)


def normalize(centres):
    master = centres.astype(jnp.float32)
    length = jnp.sqrt(jnp.sum(master * master, axis=1, keepdims=True) + EPS)
    return (master, length, master / length)


def update(master, length, unit_wide, grad_unit, momentum):
    radial = jnp.sum(unit_wide * grad_unit, axis=1, keepdims=True)
    grad_centre = (grad_unit - unit_wide * radial) / length
    velocity = MOMENTUM_RATE * momentum.astype(jnp.float32) + grad_centre + DECAY * master
    return ((master - LEARN_RATE * velocity).astype(jnp.bfloat16), velocity.astype(jnp.bfloat16))


def fold_faces(pieces, folder, start_carry):
    grouped = jax.tree.map(
        lambda part, own: part.astype(own.dtype),
        lax.all_gather(as_sent(pieces), "cls", axis=0, tiled=True),
        pieces,
    )
    return folder(
        start_carry,
        jax.tree.map(lambda part: lax.all_gather(part, "dp", axis=0, tiled=True), as_sent(grouped)),
        jnp.int32(0),
    )


def spread_back(term, face_rows):
    group_rows = lax.psum_scatter(
        term(jnp.int32(0), face_rows * lax.axis_size("cls") * lax.axis_size("dp")).astype(
            jnp.bfloat16
        ),
        "dp",
        scatter_dimension=0,
        tiled=True,
    ).astype(jnp.float32)
    return lax.psum_scatter(group_rows, "cls", scatter_dimension=0, tiled=True)


def local(faces, labels, centres, momentum):
    cls_rows = centres.shape[0]
    width = centres.shape[1]
    batches = faces.shape[0]
    face_rows = faces.shape[1]
    total_rows = labels.shape[1]
    master, length, unit_wide = normalize(centres)
    unit_rows = unit_wide.astype(jnp.bfloat16)
    class_ids = lax.axis_index(("dp", "cls")) * cls_rows + jnp.arange(cls_rows, dtype=jnp.int32)

    def make_fold(label_sets):

        def folder(carry, pieces, start):
            grad_unit, slope_sets = carry
            new_sets = []
            for label_set, piece, slope_set in zip(label_sets, pieces, slope_sets):
                cosine = lax.dot_general(
                    piece, unit_rows, (((1,), (1,)), ((), ())), preferred_element_type=jnp.float32
                )
                positive = label_set[:, None] == class_ids[None, :]
                dlogit = logit_grad(cosine, positive)
                grad_unit = grad_unit + lax.dot_general(
                    dlogit, piece, (((0,), (0,)), ((), ())), preferred_element_type=jnp.float32
                )
                new_sets.append(dlogit)
            return (grad_unit, tuple(new_sets))

        return folder

    empty_grad = jnp.zeros((cls_rows, width), jnp.float32)
    empty_slope = jnp.zeros((total_rows, cls_rows), jnp.bfloat16)
    face_sets = tuple((faces[batch_number] for batch_number in range(batches)))
    label_sets = tuple((labels[batch_number] for batch_number in range(batches)))
    empty_sets = tuple((empty_slope for batch_number in range(batches)))
    grad_unit, slope_sets = fold_faces(face_sets, make_fold(label_sets), (empty_grad, empty_sets))

    def term(start, count):
        return jnp.concatenate(
            [
                jnp.dot(slope_set, unit_rows, preferred_element_type=jnp.float32)
                for slope_set in slope_sets
            ],
            axis=1,
        )

    joined = spread_back(term, face_rows)
    face_grad = joined.reshape(face_rows, batches, width).transpose(1, 0, 2)
    new_centres, new_momentum = update(master, length, unit_wide, grad_unit, momentum)
    return (face_grad, new_centres, new_momentum)


def solution(mesh):
    in_specs = (P(None, ("dp", "cls"), None), P(), P(("dp", "cls"), None), P(("dp", "cls"), None))
    out_specs = (P(None, ("dp", "cls"), None), P(("dp", "cls"), None), P(("dp", "cls"), None))
    return jax.shard_map(local, mesh=mesh, in_specs=in_specs, out_specs=out_specs, check_vma=False)
```

profile of v0, /device:TPU:0, one launch (start us, length us, event | category | flops | bytes accessed | tf_op | source)
XLA Modules:
  0.0 139.6 jit_solution(18151039587848830202)
XLA Ops:
  7.2 0.0 reduce-scatter.2.cloned.1.call-start
  7.2 0.0 copy-start.2
  7.2 0.7 copy-done.2
  7.9 0.0 copy-start.1
  7.9 0.7 copy-done.1
  8.6 27.9 %all-gather = bf16[8,1,512]{2,1,0:T(2,128)(2,1)S(1)} all-gather(bf16[1,1,512]{2,1,0:T(2,128)(2,1)S(1)} %get-tuple-element.14), channel_id=2, replica_groups=mesh['dp'=4,'cls'=8] {'cls'}, dimensions={0}, use_global_device_ids=true | all-gather | bytes 9216 | tf_op jit(solution)/shard_map/all_gather | solution.py:49
  36.5 26.1 %all-gather.2 = bf16[8,1,512]{2,1,0:T(2,128)(2,1)S(1)} all-gather(bf16[1,1,512]{2,1,0:T(2,128)(2,1)S(1)} %get-tuple-element.15), channel_id=4, replica_groups=mesh['dp'=4,'cls'=8] {'cls'}, dimensions={0}, use_global_device_ids=true | all-gather | bytes 9216 | tf_op jit(solution)/shard_map/all_gather | solution.py:49
  62.6 5.2 %all-gather.3 = bf16[32,1,512]{2,0,1:T(8,128)(2,1)S(1)} all-gather(bf16[8,1,512]{2,0,1:T(8,128)(2,1)S(1)} %copy.23), channel_id=5, replica_groups=mesh['dp'=4,'cls'=8] {'dp'}, dimensions={0}, use_global_device_ids=true | all-gather | bytes 40960 | tf_op jit(solution)/shard_map/all_gather | solution.py:54
  67.8 5.2 %all-gather.1 = bf16[32,1,512]{2,0,1:T(8,128)(2,1)S(1)} all-gather(bf16[8,1,512]{2,0,1:T(8,128)(2,1)S(1)} %copy.21), channel_id=3, replica_groups=mesh['dp'=4,'cls'=8] {'dp'}, dimensions={0}, use_global_device_ids=true | all-gather | bytes 40960 | tf_op jit(solution)/shard_map/all_gather | solution.py:54
  73.0 1.3 copy.19
  74.2 0.2 fusion.2
  74.4 0.1 fusion.5
  74.5 0.3 fusion.9
  74.8 0.2 convolution_convert_fusion
  75.0 0.3 fusion.7
  75.3 0.2 convolution_convert_fusion.1
  75.5 0.6 pad_maximum_fusion
  76.2 0.0 reduce-scatter.2.cloned.1.call-update
  76.2 0.0 copy-start
  76.2 0.3 fusion.12
  76.6 0.7 copy-done
  77.2 0.2 copy.24
  77.5 0.4 multiply_reduce_fusion
  77.9 0.4 fusion.15
  78.2 0.2 fusion.4
  78.5 1.0 copy.27
  79.5 1.0 copy.26
  80.5 0.0 copy-start.3
  80.5 0.7 copy-done.3
  81.1 0.6 dynamic-slice
  81.7 12.1 %reduce-scatter.2.cloned.1.call-done = bf16[8,1024]{1,0:T(8,128)(2,1)} async-done(((bf16[32,1024]{1,0:T(8,128)(2,1)}), bf16[8,1024]{1,0:T(8,128)(2,1)}) %reduce-scatter.2.cloned.1.call-update) | async-done | bytes 16400 | tf_op jit(solution)/shard_map/reduce_scatter | solution.py:60
  93.8 37.8 %all-reduce = f32[8,1024]{1,0:T(8,128)S(1)} all-reduce(bf16[8,1024]{1,0:T(8,128)(2,1)} %reduce-scatter.2.cloned.1.call-done), channel_id=7, replica_groups=mesh['dp'=4,'cls'=8] {'cls'}, use_global_device_ids=true, to_apply=%region_2.3.clone | all-reduce | flops 8192 | bytes 49152
  131.6 1.2 constant_dynamic-slice_fusion
  (6 shorter events, 0.0 us)
Async XLA Ops:
  7.2 86.6 %reduce-scatter.2.cloned.1.call-start = ((), (), s32[]{:S(2)}) async-start(), calls=%async_computation.1 | async-start | bytes 81920 | tf_op jit(solution)/shard_map/reduce_scatter | solution.py:60
  7.2 0.7 copy-start.2
  7.9 0.7 copy-start.1
  76.2 1.0 copy-start
  80.5 0.7 copy-start.3
Sparse Core Ops, SparseCore 0:
  76.3 17.4 reduce-scatter.1
where the time goes:
time: 140 us
  blocking collectives  102 us (73%)
  between operations  14.1 us (10%)
  waiting for transfers between devices  12.1 us (9%)
  local copies, waits for them, and re-layouts  7.99 us (6%)
  matrix products  1.74 us (1%)
  other arithmetic  1.51 us (1%)
    all_gather x2, blocking collectives, fold_faces(): lax.all_gather(as_sent(pieces), 'cls', axis=0, tiled=True)  54 us
    unnamed x1, blocking collectives  37.8 us
    reduce_scatter x1, waiting for transfers between devices, spread_back(): lax.psum_scatter(term(jnp.int32(0), face_rows * lax.axis_size('cls') * la...  12.1 us
    all_gather x2, blocking collectives, fold_faces(): lax.all_gather(part, 'dp', axis=0, tiled=True)  10.3 us
    unnamed x15, local copies, waits for them, and re-layouts  7.98 us
  transfers between devices with their start and end apart: 1, of which 1 were waited for; matrix products, arithmetic and copies ran while one was open for 3% of the time, Pallas kernels for 0%

commit v1 on v0

--- a/solution.py
+++ b/solution.py
@@ -11,6 +11,18 @@
 MOMENTUM_RATE = 0.9
 LEARN_RATE = 0.1
 DECAY = 0.0005
+
+
+def gather_by_bits(array, axis, dim):
+    ways, here = (lax.axis_size(axis), lax.axis_index(axis))
+    grown, reach = (array, 1)
+    while reach < ways:
+        theirs = lax.ppermute(grown, axis, [(d, d ^ reach) for d in range(ways)])
+        mine_first = jnp.concatenate([grown, theirs], axis=dim)
+        theirs_first = jnp.concatenate([theirs, grown], axis=dim)
+        grown = jnp.where(here & reach == 0, mine_first, theirs_first)
+        reach = 2 * reach
+    return grown
 
 
 def as_sent(x):
@@ -51,7 +63,7 @@
     )
     return folder(
         start_carry,
-        jax.tree.map(lambda part: lax.all_gather(part, "dp", axis=0, tiled=True), as_sent(grouped)),
+        jax.tree.map(lambda part: gather_by_bits(part, "dp", 0), as_sent(grouped)),
         jnp.int32(0),
     )
 

time: 140 us -> 136 us (0.971)
  blocking collectives: 102 us -> 91.8 us
  waiting for transfers between devices: 12.1 us -> 16.1 us
  starting transfers between devices: 0.04 us -> 2.2 us
    all_gather x2 -> x0, blocking collectives: 10.3 us -> none  [fold_faces(): lax.all_gather(part, 'dp', axis=0, tiled=True)]
    ppermute x0 -> x4, waiting for transfers between devices: none -> 2.71 us  [gather_by_bits(): theirs = lax.ppermute(grown, axis, [(d, d ^ reach) for d in range(ways)])]
    ppermute x0 -> x4, starting transfers between devices: none -> 2.16 us  [gather_by_bits(): theirs = lax.ppermute(grown, axis, [(d, d ^ reach) for d in range(ways)])]
  transfers between devices with their start and end apart: 1 -> 5, of which waited for: 1 -> 3; matrix products, arithmetic and copies ran while one was open for 3% -> 4% of each run, Pallas kernels for 0% -> 0%
where the time goes in v1:
time: 136 us
  blocking collectives  91.8 us (68%)
  waiting for transfers between devices  16.1 us (12%)
  between operations  14.2 us (10%)
  local copies, waits for them, and re-layouts  8.2 us (6%)
  starting transfers between devices  2.2 us (2%)
  matrix products  1.72 us (1%)
  other arithmetic  1.46 us (1%)
    all_gather x2, blocking collectives, fold_faces(): lax.all_gather(as_sent(pieces), 'cls', axis=0, tiled=True)  54 us
    unnamed x1, blocking collectives  37.7 us
    reduce_scatter x1, waiting for transfers between devices, spread_back(): lax.psum_scatter(term(jnp.int32(0), face_rows * lax.axis_size('cls') * la...  13.4 us
    unnamed x15, local copies, waits for them, and re-layouts  8.2 us
  transfers between devices with their start and end apart: 5, of which 3 were waited for; matrix products, arithmetic and copies ran while one was open for 4% of the time, Pallas kernels for 0%

profile of v1, /device:TPU:0, one launch (start us, length us, event | category | flops | bytes accessed | tf_op | source)
XLA Modules:
  0.0 135.6 jit_solution(6765676139747799770)
XLA Ops:
  7.2 0.0 reduce-scatter.2.cloned.1.call-start
  7.2 0.8 slice_bitcast_fusion.1
  8.0 27.9 %all-gather.1 = bf16[8,1,512]{2,1,0:T(2,128)(2,1)S(1)} all-gather(bf16[1,1,512]{2,1,0:T(2,128)(2,1)S(1)} %get-tuple-element.15), channel_id=3, replica_groups=mesh['dp'=4,'cls'=8] {'cls'}, dimensions={0}, use_global_device_ids=true | all-gather | bytes 9216 | tf_op jit(solution)/shard_map/all_gather | solution.py:61
  35.9 0.0 collective-permute-start.2
  35.9 26.1 %all-gather = bf16[8,1,512]{2,1,0:T(2,128)(2,1)S(1)} all-gather(bf16[1,1,512]{2,1,0:T(2,128)(2,1)S(1)} %get-tuple-element.14), channel_id=2, replica_groups=mesh['dp'=4,'cls'=8] {'cls'}, dimensions={0}, use_global_device_ids=true | all-gather | bytes 9216 | tf_op jit(solution)/shard_map/all_gather | solution.py:61
  62.0 0.0 collective-permute-start
  62.0 0.0 copy-start.1
  62.1 0.7 copy-done.1
  62.7 1.3 copy.20
  64.0 0.2 fusion
  64.2 0.0 copy-start
  64.2 0.1 fusion.3
  64.3 0.9 copy-done
  65.2 0.2 copy.22
  65.4 0.0 copy-start.2
  65.4 0.6 copy-done.2
  66.1 0.6 dynamic-slice
  66.7 0.0 collective-permute-done
  66.7 1.6 %collective-permute-start.1 = (bf16[16,512]{1,0:T(8,128)(2,1)S(1)}, bf16[16,512]{1,0:T(8,128)(2,1)S(1)}, u32[]{:S(2)}, u32[]{:S(2)}) collective-permute-start(bf16[16,512]{1,0:T(8,128)(2,1)S(1)} %maximum_select_fusion.2), channel_id=1, source_target_pairs={{0,16},{8,24},{16,0},{24,8},{1,17},{9,25},{17,1},{25,9},{2,18},{10... | collective-permute-start | bytes 49160 | tf_op jit(solution)/shard_map/ppermute | solution.py:20
  68.2 0.0 collective-permute-done.2
  68.2 0.6 collective-permute-start.3
  68.8 1.6 %collective-permute-done.1 = bf16[16,512]{1,0:T(8,128)(2,1)S(1)} collective-permute-done((bf16[16,512]{1,0:T(8,128)(2,1)S(1)}, bf16[16,512]{1,0:T(8,128)(2,1)S(1)}, u32[]{:S(2)}, u32[]{:S(2)}) %collective-permute-start.1) | collective-permute-done | bytes 16416 | tf_op jit(solution)/shard_map/ppermute | solution.py:20
  70.5 0.2 fusion.5
  70.7 0.2 convolution_convert_fusion.1
  71.0 1.1 collective-permute-done.3
  72.0 0.3 fusion.7
  72.3 0.3 convolution_convert_fusion
  72.6 0.6 pad_maximum_fusion
  73.2 0.0 reduce-scatter.2.cloned.1.call-update
  73.2 0.3 fusion.8
  73.6 0.4 multiply_reduce_fusion
  73.9 0.4 fusion.13
  74.3 0.2 fusion.2
  74.5 1.0 copy.25
  75.5 1.0 copy.24
  76.5 13.4 %reduce-scatter.2.cloned.1.call-done = bf16[8,1024]{1,0:T(8,128)(2,1)} async-done(((bf16[32,1024]{1,0:T(8,128)(2,1)}), bf16[8,1024]{1,0:T(8,128)(2,1)}) %reduce-scatter.2.cloned.1.call-update) | async-done | bytes 16400 | tf_op jit(solution)/shard_map/reduce_scatter | solution.py:72
  89.9 37.7 %all-reduce = f32[8,1024]{1,0:T(8,128)S(1)} all-reduce(bf16[8,1024]{1,0:T(8,128)(2,1)} %reduce-scatter.2.cloned.1.call-done), channel_id=5, replica_groups=mesh['dp'=4,'cls'=8] {'cls'}, use_global_device_ids=true, to_apply=%region_2.3.clone | all-reduce | flops 8192 | bytes 49152
  127.6 1.2 constant_dynamic-slice_fusion
  (7 shorter events, 0.0 us)
Async XLA Ops:
  7.2 82.7 %reduce-scatter.2.cloned.1.call-start = ((), (), s32[]{:S(2)}) async-start(), calls=%async_computation.1 | async-start | bytes 81920 | tf_op jit(solution)/shard_map/reduce_scatter | solution.py:72
  35.9 32.3 %collective-permute-start.2 = (bf16[8,512]{1,0:T(8,128)(2,1)S(1)}, bf16[8,512]{1,0:T(8,128)(2,1)S(1)}, u32[]{:S(2)}, u32[]{:S(2)}) collective-permute-start(bf16[8,512]{1,0:T(8,128)(2,1)S(1)} %bitcast.24), channel_id=1, source_target_pairs={{0,8},{8,0},{16,24},{24,16},{1,9},{9,1},{17,25},{25,17},{2,10},{10... | collective-permute-start | bytes 24584 | tf_op jit(solution)/shard_map/ppermute | solution.py:20
  62.0 4.6 %collective-permute-start = (bf16[8,512]{1,0:T(8,128)(2,1)S(1)}, bf16[8,512]{1,0:T(8,128)(2,1)S(1)}, u32[]{:S(2)}, u32[]{:S(2)}) collective-permute-start(bf16[8,512]{1,0:T(8,128)(2,1)S(1)} %bitcast.26), channel_id=1, source_target_pairs={{0,8},{8,0},{16,24},{24,16},{1,9},{9,1},{17,25},{25,17},{2,10},{10... | collective-permute-start | bytes 24584 | tf_op jit(solution)/shard_map/ppermute | solution.py:20
  62.0 0.7 copy-start.1
  64.2 1.0 copy-start
  65.4 0.7 copy-start.2
  66.7 3.8 %collective-permute-start.1 = (bf16[16,512]{1,0:T(8,128)(2,1)S(1)}, bf16[16,512]{1,0:T(8,128)(2,1)S(1)}, u32[]{:S(2)}, u32[]{:S(2)}) collective-permute-start(bf16[16,512]{1,0:T(8,128)(2,1)S(1)} %maximum_select_fusion.2), channel_id=1, source_target_pairs={{0,16},{8,24},{16,0},{24,8},{1,17},{9,25},{17,1},{25,9},{2,18},{10... | collective-permute-start | bytes 49160 | tf_op jit(solution)/shard_map/ppermute | solution.py:20
  68.2 3.8 %collective-permute-start.3 = (bf16[16,512]{1,0:T(8,128)(2,1)S(1)}, bf16[16,512]{1,0:T(8,128)(2,1)S(1)}, u32[]{:S(2)}, u32[]{:S(2)}) collective-permute-start(bf16[16,512]{1,0:T(8,128)(2,1)S(1)} %maximum_select_fusion.3), channel_id=1, source_target_pairs={{0,16},{8,24},{16,0},{24,8},{1,17},{9,25},{17,1},{25,9},{2,18},{10... | collective-permute-start | bytes 49160 | tf_op jit(solution)/shard_map/ppermute | solution.py:20
Sparse Core Ops, SparseCore 0:
  73.3 16.5 reduce-scatter.1
